TPU v7x, 32 devices: a whole 2x2x4 slice. The times are simulated.
32 devices in a mesh: energy: 4 (over y, x), kmom: 8 (over z, core).
Axes of the slice: x: 2, y: 2, z: 4, core: 2. Of those that a mesh axis runs over, the one named last changes fastest.
Arguments:
- green_blocks: bfloat16 [8, 8, 144, 1024], P('energy', 'kmom'), may hold values from -6 to 6
- phonon: float32 [2, 8, 8], replicated, may hold values from -0.4 to 0.4
- offsets: int32 [8], replicated, may hold values from 1 to 2, as said below
- neighbours: int32 [1024, 8], P('kmom'), may hold values from 0 to 1023, as said below
- coupling: float32 [8, 12, 12], replicated, may hold values from -1.75 to 1.75
Outputs:
- self_energy: bfloat16 [8, 8, 144, 1024], P('energy', 'kmom')
Inputs may be any that keep to these rules, and one draw needn't show every extreme that they name: `offsets`: each value lies in 1 .. 2; at least one equals 2. Every neighbour of atom a lies within 32 of a in index; some atom has neighbours at exactly a + 32 and a - 32.
All inputs are finite; a program needn't handle non-finite values.
Results may differ from a plain program's by a relative error of at most 0.0064.
Values may be sent and summed in bfloat16 or wider, within the bound.
A program may use at most 64 MiB of HBM per device.

v0:
```python
import functools

import jax
import jax.numpy as jnp
import numpy as np
from jax import lax
from jax.experimental import pallas as pl
from jax.experimental.pallas import tpu as pltpu
from jax.sharding import PartitionSpec as P

OFFSET = 2
RADIUS = 32
ROWS = 16
EARLY = 7
MESH = pl.DeviceIdType.MESH


def spread_ones(slots, orbs):
    col = np.arange(slots * orbs * orbs)
    row = np.arange(slots * orbs)[:, None]
    first = row == col // orbs
    second = row == (col // (orbs * orbs)) * orbs + col % orbs
    return jnp.asarray(np.concatenate([first, second], axis=1), jnp.bfloat16)


def fill_maps(coupling, ones, maps_wide, maps):
    orbs, slots = coupling.shape[0], coupling.shape[1]
    count = slots * orbs * orbs
    blocks = jnp.concatenate([coupling[:, slot, :] for slot in range(slots)], axis=1)
    high = blocks.astype(jnp.bfloat16)
    rest = blocks - high.astype(jnp.float32)
    mid = rest.astype(jnp.bfloat16)
    low = (rest - mid.astype(jnp.float32)).astype(jnp.bfloat16)
    both = sum(
        jnp.dot(term, ones[...], preferred_element_type=jnp.float32) for term in (high, mid, low)
    )
    left, right = both[:, :count], both[:, count:]
    for orb in range(orbs):
        maps_wide[orb * orbs : (orb + 1) * orbs, :] = left[orb : orb + 1, :] * right
    maps[...] = maps_wide[...].astype(jnp.bfloat16)


def small_kernel(phonon, offsets, block_rows):
    freqs, moms = phonon.shape[1], phonon.shape[2]
    flat = moms * block_rows
    place = lax.broadcasted_iota(jnp.int32, (freqs, moms), 0)
    shift = jnp.zeros((freqs, moms), jnp.int32)
    for freq in range(freqs):
        shift = jnp.where(place == freq, offsets[freq], shift)
    row = lax.broadcasted_iota(jnp.int32, (flat, 3 * flat), 0)
    col = lax.broadcasted_iota(jnp.int32, (flat, 3 * flat), 1)
    mom_diff = (row // block_rows - (col // block_rows) % moms + moms) % moms
    tile = (col >= flat).astype(jnp.int32) + (col >= 2 * flat).astype(jnp.int32)
    rel = block_rows * (tile - 1) + col % block_rows - row % block_rows
    small = jnp.zeros((flat, 3 * flat), jnp.float32)
    for step in range(-OFFSET, OFFSET + 1):
        terms = [
            jnp.where((2 * sign - 1) * shift == step, phonon[sign], 0.0) for sign in (0, 1)
        ]
        taps = jnp.sum(terms[0] + terms[1], axis=0, keepdims=True)
        code = jnp.where(rel == step, mom_diff, -1)
        for mom in range(moms):
            small = jnp.where(code == mom, taps[:, mom : mom + 1], small)
    return small.astype(jnp.bfloat16)


def fill_wide(small, wide):
    flat = small.shape[0]
    grow = (
        lax.broadcasted_iota(jnp.int32, (flat * ROWS, flat), 0) // ROWS
        == lax.broadcasted_iota(jnp.int32, (flat * ROWS, flat), 1)
    )
    tall = jnp.dot(
        jnp.where(grow, 1.0, 0.0).astype(jnp.bfloat16), small, preferred_element_type=jnp.float32
    ).astype(jnp.bfloat16)
    for part in range(3):
        span = flat * ROWS
        spread = (
            lax.broadcasted_iota(jnp.int32, (flat, span), 1) // ROWS
            == lax.broadcasted_iota(jnp.int32, (flat, span), 0)
        )
        full = jnp.dot(
            tall[:, part * flat : (part + 1) * flat],
            jnp.where(spread, 1.0, 0.0).astype(jnp.bfloat16),
            preferred_element_type=jnp.float32,
        )
        same = (
            lax.broadcasted_iota(jnp.int32, (span, span), 0) % ROWS
            == lax.broadcasted_iota(jnp.int32, (span, span), 1) % ROWS
        )
        wide[:, part * span : (part + 1) * span] = jnp.where(same, full, 0.0).astype(jnp.bfloat16)


def paired(index, step, count):
    if count & (count - 1):
        return lax.rem(index + step, count)
    total = jnp.int32(0)
    bit = 1
    while bit < count:
        total = total + lax.rem(lax.div(index, bit) + lax.div(step, bit), 2) * bit
        bit *= 2
    return total


def kernel(
    sizes, green, near, phonon, offsets, coupling, ones, out,
    maps_wide, maps, near_all, taken, coupled, wide, recv, res,
    near_send, near_recv, in_send, in_recv, out_send, out_recv,
):
    ne, nk, window = sizes
    block_rows, pairs, atoms = green.shape
    slots, group = near.shape
    tiles = pairs // ROWS
    rounds = recv.shape[0]
    my_e = lax.axis_index("energy")
    my_k = lax.axis_index("kmom")

    barrier = pltpu.get_barrier_semaphore()

    def greet(i, _):
        other_e = lax.div(i, nk)
        other_k = lax.rem(i, nk)

        @pl.when((other_e != my_e) | (other_k != my_k))
        def _():
            pl.semaphore_signal(barrier, inc=1, device_id=(other_e, other_k), device_id_type=MESH)

        return 0

    lax.fori_loop(0, ne * nk, greet, 0)
    small = small_kernel(phonon, offsets, block_rows)
    fill_wide(small, wide)
    fill_maps(coupling, ones, maps_wide, maps)
    flat = small.shape[0]

    def near_copy(i):
        other = paired(my_k, i, nk)
        return pltpu.make_async_remote_copy(
            src_ref=near, dst_ref=near_all.at[my_k], send_sem=near_send, recv_sem=near_recv.at[my_k],
            device_id=(my_e, other), device_id_type=MESH,
        )

    def all_others(act):
        def step(i, _):
            act(i)
            return 0

        lax.fori_loop(1, nk, step, 0)

    def in_copies(tile, grp, start):
        turn, step = tile // ne, tile % ne
        count = min(ne, tiles - turn * ne)
        if count == ne:
            target, target_k = jnp.int32(step), lax.rem(grp + step * nk // ne + turn, nk)
        else:
            target, target_k = lax.rem(step + count * grp, ne), grp
        src = coupled.at[:, pl.ds(tile * ROWS, ROWS), pl.ds(pl.multiple_of(grp * group, 128), group)]
        dst = recv.at[turn, my_e, my_k]
        own = (target == my_e) & (target_k == my_k)

        @pl.when(jnp.logical_not(own))
        def _():
            copy = pltpu.make_async_remote_copy(
                src_ref=src, dst_ref=dst, send_sem=in_send, recv_sem=in_recv.at[turn],
                device_id=(target, target_k), device_id_type=MESH,
            )
            if start:
                copy.start()
            else:
                copy.wait_send()

        if start:
            @pl.when(own)
            def _():
                pltpu.make_async_copy(src, dst, in_recv.at[turn]).start()

    def couple(grp, index):
        base = pl.multiple_of(jnp.clip((grp - 1) * group, 0, atoms - window), 128)
        index = index - base
        source = green[:, :, pl.ds(base, window)].reshape(block_rows * pairs, window)
        places = lax.broadcasted_iota(jnp.int32, (window, group), 0)
        for first in range(0, slots, 2):
            hits = [
                jnp.where(places == index[slot : slot + 1, :], 1.0, 0.0).astype(jnp.bfloat16)
                for slot in (first, first + 1)
            ]
            got = jnp.dot(
                source, jnp.concatenate(hits, axis=1), preferred_element_type=jnp.float32
            ).astype(jnp.bfloat16)
            for slot in (first, first + 1):
                for row in range(block_rows):
                    taken[slot * pairs : (slot + 1) * pairs, row * group : (row + 1) * group] = got[
                        row * pairs : (row + 1) * pairs,
                        (slot - first) * group : (slot - first + 1) * group,
                    ]
        total = jnp.dot(maps[...], taken[...], preferred_element_type=jnp.float32).astype(jnp.bfloat16)
        lanes = pl.ds(pl.multiple_of(grp * group, 128), group)
        for row in range(block_rows):
            coupled[row, :, lanes] = total[:, row * group : (row + 1) * group]

    early = tiles if rounds == 1 else EARLY

    def send_early(grp):
        for tile in range(early):
            in_copies(tile, grp, True)

    couple(my_k, near[...])
    pl.semaphore_wait(barrier, ne * nk - 1)
    all_others(lambda i: near_copy(i).start())
    send_early(my_k)

    def couple_other(i, _):
        grp = paired(my_k, i, nk)
        pltpu.make_async_remote_copy(
            src_ref=near, dst_ref=near_all.at[grp], send_sem=near_send, recv_sem=near_recv.at[grp],
            device_id=(my_e, grp), device_id_type=MESH,
        ).wait_recv()
        couple(grp, near_all[grp])
        send_early(grp)
        return 0

    lax.fori_loop(1, nk, couple_other, 0)

    def send_late(i, _):
        grp = paired(my_k, i, nk)
        for tile in range(early, tiles):
            in_copies(tile, grp, True)
        return 0

    lax.fori_loop(0, nk, send_late, 0)

    def mine(turn):
        count = min(ne, tiles - turn * ne)
        if count == ne:
            return my_e, lax.rem(my_k + 2 * nk - lax.div(my_e * nk, ne) - turn, nk)
        return lax.rem(my_e + count * (ne - 1) * my_k, ne), my_k

    def out_copies(turn, start, places=tuple(range(ne))):
        step_of, grp_of = mine(turn)
        tile = step_of + turn * ne
        dst = out.at[
            :, pl.ds(pl.multiple_of(tile * ROWS, ROWS), ROWS), pl.ds(pl.multiple_of(grp_of * group, 128), group)
        ]

        def step(i, _):
            target = paired(my_k, i, nk)
            for other in places:
                src = res.at[turn, other, target]
                own = (other == my_e) & (target == my_k)

                @pl.when(jnp.logical_not(own))
                def _(src=src, other=other):
                    copy = pltpu.make_async_remote_copy(
                        src_ref=src, dst_ref=dst, send_sem=out_send, recv_sem=out_recv,
                        device_id=(jnp.int32(other), target), device_id_type=MESH,
                    )
                    if start:
                        copy.start()
                    else:
                        copy.wait_send()

                if start:
                    @pl.when(own)
                    def _(src=src):
                        pltpu.make_async_copy(src, dst, out_recv).start()
            return 0

        lax.fori_loop(0, nk, step, 0)

    def finish(turn):
        pltpu.make_async_copy(recv.at[turn], recv.at[turn], in_recv.at[turn]).wait()
        span = flat * ROWS
        for place in range(ne):
            low, high = max(place - 1, 0), min(place + 1, ne - 1)
            piece = recv[turn, low : high + 1].reshape((high - low + 1) * span, group)
            value = jnp.dot(
                wide[:, (low - place + 1) * span : (high - place + 2) * span],
                piece,
                preferred_element_type=jnp.float32,
            )
            res[turn, place] = value.astype(jnp.bfloat16).reshape(nk, block_rows, ROWS, group)
            out_copies(turn, True, (place,))

    def each_turn(act):
        for turn in range(rounds):
            if turn * ne + ne <= tiles:
                act(turn)
            else:
                @pl.when(mine(turn)[0] + turn * ne < tiles)
                def _(turn=turn):
                    act(turn)

    each_turn(finish)

    pltpu.make_async_copy(out, out, out_recv).wait()
    all_others(lambda i: near_copy(i).wait_send())

    def drain(i, _):
        grp = paired(my_k, i, nk)
        for tile in range(tiles):
            in_copies(tile, grp, False)
        return 0

    lax.fori_loop(0, nk, drain, 0)
    each_turn(lambda turn: out_copies(turn, False))


def body(ne, nk, green_blocks, phonon, offsets, neighbours, coupling):
    block_rows, _, pairs, atoms = green_blocks.shape
    group, slots = neighbours.shape
    rounds = -(-(pairs // ROWS) // ne)
    window = min(3 * group, atoms)
    flat = nk * block_rows
    vmem = pl.BlockSpec(memory_space=pltpu.VMEM)
    block = (block_rows, ROWS, group)
    result = pl.pallas_call(
        functools.partial(kernel, (ne, nk, window)),
        out_shape=pltpu.VMEM((block_rows, pairs, atoms), jnp.bfloat16),
        in_specs=[vmem, vmem, vmem, pl.BlockSpec(memory_space=pltpu.SMEM), vmem, vmem],
        out_specs=vmem,
        scratch_shapes=[
            pltpu.VMEM((pairs, slots * pairs), jnp.float32),
            pltpu.VMEM((pairs, slots * pairs), jnp.bfloat16),
            pltpu.VMEM((nk, slots, group), jnp.int32),
            pltpu.VMEM((slots * pairs, block_rows * group), jnp.bfloat16),
            pltpu.VMEM((block_rows, pairs, atoms), jnp.bfloat16),
            pltpu.VMEM((flat * ROWS, 3 * flat * ROWS), jnp.bfloat16),
            pltpu.VMEM((rounds, ne, nk) + block, jnp.bfloat16),
            pltpu.VMEM((rounds, ne, nk) + block, jnp.bfloat16),
            pltpu.SemaphoreType.DMA,
            pltpu.SemaphoreType.DMA((nk,)),
            pltpu.SemaphoreType.DMA,
            pltpu.SemaphoreType.DMA((rounds,)),
            pltpu.SemaphoreType.DMA,
            pltpu.SemaphoreType.DMA,
        ],
        compiler_params=pltpu.CompilerParams(collective_id=0, has_side_effects=True),
    )(
        green_blocks.reshape(block_rows, pairs, atoms),
        neighbours.T,
        phonon,
        offsets,
        coupling.transpose(1, 0, 2),
        spread_ones(slots, coupling.shape[1]),
    )
    return result.reshape(green_blocks.shape)


def solution(mesh):
    placed = (P("energy", "kmom", None, None), P(), P(), P("kmom", None), P())
    return jax.shard_map(
        functools.partial(body, mesh.shape["energy"], mesh.shape["kmom"]),
        mesh=mesh, in_specs=placed, out_specs=P("energy", "kmom", None, None), check_vma=False,
    )
```

profile of v0, /device:TPU:0, one launch (start us, length us, event | category | flops | bytes accessed | tf_op | source)
XLA Modules:
  0.0 36.5 jit_solution(6327403435522907371)
XLA Ops:
  0.0 35.7 %shard_map.64 = bf16[2,144,1024]{2,1,0:T(8,128)(2,1)S(1)} custom-call(bf16[2,144,1024]{2,1,0:T(8,128)(2,1)} %bitcast.7, s32[8,128]{1,0:T(8,128)} %bitcast.9, f32[2,8,8]{2,1,0:T(8,128)} %phonon.1, s32[8]{0:T(128)} %offsets.1, f32[12,8,12]{2,1,0:T(8,128)} %bitcast.8, bf16[96,2304]{1,0:T(8,128)(2,1)} %constant.2.clone.ones), custom_call_target="tpu_custom_call" | custom-call | tf_op jit(solution)/shard_map/pallas_call | solution.py:316
  35.7 0.8 %copy.9 = bf16[2,1,144,1024]{3,2,1,0:T(8,128)(2,1)} copy(bf16[2,1,144,1024]{3,2,1,0:T(8,128)(2,1)S(1)} %bitcast.6) | data formatting | bytes 1179648
where the time goes:
time: 36.6 us; the launch traced here: 36.5 us
  Pallas kernels  35.7 us (98%)
  local copies, waits for them, and re-layouts  0.82 us (2%)
    pallas_call x1, Pallas kernels, body(): pl.pallas_call(functools.partial(kernel, (ne, nk, window)), out_shape=plt...  35.7 us
    unnamed x1, local copies, waits for them, and re-layouts  0.82 us

commit v1 on v0

--- a/solution.py
+++ b/solution.py
@@ -91,6 +91,11 @@
         wide[:, part * span : (part + 1) * span] = jnp.where(same, full, 0.0).astype(jnp.bfloat16)
 
 
+def SCOPE(name, act):
+    with jax.named_scope(name):
+        act()
+
+
 def paired(index, step, count):
     if count & (count - 1):
         return lax.rem(index + step, count)
@@ -103,9 +108,9 @@
 
 
 def kernel(
-    sizes, green, near, phonon, offsets, coupling, ones, out,
-    maps_wide, maps, near_all, taken, coupled, wide, recv, res,
-    near_send, near_recv, in_send, in_recv, out_send, out_recv,
+    sizes, green_any, near_any, phonon_any, offsets_any, coupling_any, ones_any, out,
+    green, near, phonon, offsets, coupling, ones, maps_wide, maps, near_all, taken, coupled, wide, recv, res,
+    load_sem, near_send, near_recv, in_send, in_recv, out_send, out_recv,
 ):
     ne, nk, window = sizes
     block_rows, pairs, atoms = green.shape
@@ -116,22 +121,31 @@
     my_k = lax.axis_index("kmom")
 
     barrier = pltpu.get_barrier_semaphore()
+    loads = [
+        pltpu.make_async_copy(src, dst, load_sem.at[i])
+        for i, (src, dst) in enumerate(
+            [
+                (coupling_any, coupling), (ones_any, ones), (near_any, near), (green_any, green),
+                (phonon_any, phonon), (offsets_any, offsets),
+            ]
+        )
+    ]
+    for load in loads[:2]:
+        load.start()
 
     def greet(i, _):
-        other_e = lax.div(i, nk)
-        other_k = lax.rem(i, nk)
-
-        @pl.when((other_e != my_e) | (other_k != my_k))
-        def _():
-            pl.semaphore_signal(barrier, inc=1, device_id=(other_e, other_k), device_id_type=MESH)
-
+        place = lax.rem(my_e * nk + my_k + i, ne * nk)
+        pl.semaphore_signal(
+            barrier, inc=1, device_id=(lax.div(place, nk), lax.rem(place, nk)), device_id_type=MESH
+        )
         return 0
 
-    lax.fori_loop(0, ne * nk, greet, 0)
-    small = small_kernel(phonon, offsets, block_rows)
-    fill_wide(small, wide)
-    fill_maps(coupling, ones, maps_wide, maps)
-    flat = small.shape[0]
+    SCOPE("greet", lambda: lax.fori_loop(1, ne * nk, greet, 0))
+    for load in loads[2:]:
+        load.start()
+    SCOPE("lones", lambda: [loads[0].wait(), loads[1].wait()])
+    SCOPE("maps", lambda: fill_maps(coupling, ones, maps_wide, maps))
+    flat = nk * block_rows
 
     def near_copy(i):
         other = paired(my_k, i, nk)
@@ -204,8 +218,10 @@
         for tile in range(early):
             in_copies(tile, grp, True)
 
-    couple(my_k, near[...])
-    pl.semaphore_wait(barrier, ne * nk - 1)
+    SCOPE("lgreen", lambda: [load.wait() for load in loads[2:]])
+    SCOPE("couple0", lambda: couple(my_k, near[...]))
+    SCOPE("small", lambda: fill_wide(small_kernel(phonon, offsets, block_rows), wide))
+    SCOPE("barwait", lambda: pl.semaphore_wait(barrier, ne * nk - 1))
     all_others(lambda i: near_copy(i).start())
     send_early(my_k)
 
@@ -219,7 +235,7 @@
         send_early(grp)
         return 0
 
-    lax.fori_loop(1, nk, couple_other, 0)
+    SCOPE("couples", lambda: lax.fori_loop(1, nk, couple_other, 0))
 
     def send_late(i, _):
         grp = paired(my_k, i, nk)
@@ -227,7 +243,7 @@
             in_copies(tile, grp, True)
         return 0
 
-    lax.fori_loop(0, nk, send_late, 0)
+    SCOPE("late", lambda: lax.fori_loop(0, nk, send_late, 0))
 
     def mine(turn):
         count = min(ne, tiles - turn * ne)
@@ -268,7 +284,7 @@
         lax.fori_loop(0, nk, step, 0)
 
     def finish(turn):
-        pltpu.make_async_copy(recv.at[turn], recv.at[turn], in_recv.at[turn]).wait()
+        SCOPE("turnwait%d" % turn, lambda: pltpu.make_async_copy(recv.at[turn], recv.at[turn], in_recv.at[turn]).wait())
         span = flat * ROWS
         for place in range(ne):
             low, high = max(place - 1, 0), min(place + 1, ne - 1)
@@ -292,17 +308,35 @@
 
     each_turn(finish)
 
-    pltpu.make_async_copy(out, out, out_recv).wait()
-    all_others(lambda i: near_copy(i).wait_send())
-
-    def drain(i, _):
-        grp = paired(my_k, i, nk)
-        for tile in range(tiles):
-            in_copies(tile, grp, False)
-        return 0
-
-    lax.fori_loop(0, nk, drain, 0)
-    each_turn(lambda turn: out_copies(turn, False))
+    def all_sent(block, sem, others):
+        span = block.at[pl.ds(0, others)]
+        pltpu.make_async_copy(span, span, sem).wait()
+
+    def drain(turn):
+        blocks = recv.at[turn]
+        pltpu.make_async_copy(blocks.at[pl.ds(0, ne - 1)], blocks.at[pl.ds(0, ne - 1)], out_send).wait()
+        all_sent(blocks.at[0], out_send, nk - 1)
+
+    SCOPE("outwait", lambda: pltpu.make_async_copy(out, out, out_recv).wait())
+
+    def finals():
+        each_turn(drain)
+        all_sent(near_all, near_send, nk - 1)
+        for turn in range(rounds):
+            count = min(ne, tiles - turn * ne)
+            owner = mine(turn)[0] < count
+            rows = nk * count
+            full, rest = rows // nk, rows % nk
+            first = recv.at[turn, pl.ds(0, count - 1)]
+            if count > 1:
+                pltpu.make_async_copy(first, first, in_send).wait()
+            all_sent(recv.at[turn, 0], in_send, nk - 1)
+
+            @pl.when(jnp.logical_not(owner))
+            def _(turn=turn):
+                all_sent(recv.at[turn, 0], in_send, 1)
+
+    SCOPE("finals", finals)
 
 
 def body(ne, nk, green_blocks, phonon, offsets, neighbours, coupling):
@@ -312,13 +346,22 @@
     window = min(3 * group, atoms)
     flat = nk * block_rows
     vmem = pl.BlockSpec(memory_space=pltpu.VMEM)
+    anyw = pl.BlockSpec(memory_space=pl.ANY)
+    ones = spread_ones(slots, coupling.shape[1])
+    maps_in = coupling.transpose(1, 0, 2)
     block = (block_rows, ROWS, group)
     result = pl.pallas_call(
         functools.partial(kernel, (ne, nk, window)),
         out_shape=pltpu.VMEM((block_rows, pairs, atoms), jnp.bfloat16),
-        in_specs=[vmem, vmem, vmem, pl.BlockSpec(memory_space=pltpu.SMEM), vmem, vmem],
+        in_specs=[anyw] * 6,
         out_specs=vmem,
         scratch_shapes=[
+            pltpu.VMEM((block_rows, pairs, atoms), jnp.bfloat16),
+            pltpu.VMEM((slots, group), jnp.int32),
+            pltpu.VMEM(phonon.shape, jnp.float32),
+            pltpu.SMEM(offsets.shape, jnp.int32),
+            pltpu.VMEM(maps_in.shape, jnp.float32),
+            pltpu.VMEM(ones.shape, jnp.bfloat16),
             pltpu.VMEM((pairs, slots * pairs), jnp.float32),
             pltpu.VMEM((pairs, slots * pairs), jnp.bfloat16),
             pltpu.VMEM((nk, slots, group), jnp.int32),
@@ -327,6 +370,7 @@
             pltpu.VMEM((flat * ROWS, 3 * flat * ROWS), jnp.bfloat16),
             pltpu.VMEM((rounds, ne, nk) + block, jnp.bfloat16),
             pltpu.VMEM((rounds, ne, nk) + block, jnp.bfloat16),
+            pltpu.SemaphoreType.DMA((6,)),
             pltpu.SemaphoreType.DMA,
             pltpu.SemaphoreType.DMA((nk,)),
             pltpu.SemaphoreType.DMA,
@@ -340,8 +384,8 @@
         neighbours.T,
         phonon,
         offsets,
-        coupling.transpose(1, 0, 2),
-        spread_ones(slots, coupling.shape[1]),
+        maps_in,
+        ones,
     )
     return result.reshape(green_blocks.shape)
 

time: 36.6 us -> 34.9 us (0.954)
  Pallas kernels: 35.7 us -> 33.9 us
    pallas_call x1, Pallas kernels: 35.7 us -> 33.9 us  [body(): pl.pallas_call(functools.partial(kernel, (ne, nk, window)), out_shape=plt...]
where the time goes in v1:
time: 34.9 us; the launch traced here: 34.7 us
  Pallas kernels  33.9 us (97%)
  local copies, waits for them, and re-layouts  0.82 us (2%)
    pallas_call x1, Pallas kernels, body(): pl.pallas_call(functools.partial(kernel, (ne, nk, window)), out_shape=plt...  33.9 us
    unnamed x1, local copies, waits for them, and re-layouts  0.82 us

profile of v1, /device:TPU:0, one launch (start us, length us, event | category | flops | bytes accessed | tf_op | source)
XLA Modules:
  0.0 34.7 jit_solution(14466063497655035387)
XLA Ops:
  0.0 33.9 %shard_map.64 = bf16[2,144,1024]{2,1,0:T(8,128)(2,1)S(1)} custom-call(bf16[2,144,1024]{2,1,0:T(8,128)(2,1)} %bitcast.7, s32[8,128]{1,0:T(8,128)} %bitcast.9, f32[2,8,8]{2,1,0:T(8,128)} %phonon_any.1, s32[8]{0:T(128)} %offsets_any.1, f32[12,8,12]{2,1,0:T(8,128)} %bitcast.8, bf16[96,2304]{1,0:T(8,128)(2,1)} %constant.2.clone.ones_any), custom_call_target="tpu_custom_call" | custom-call | tf_op jit(solution)/shard_map/pallas_call | solution.py:353
  33.9 0.8 %copy.9 = bf16[2,1,144,1024]{3,2,1,0:T(8,128)(2,1)} copy(bf16[2,1,144,1024]{3,2,1,0:T(8,128)(2,1)S(1)} %bitcast.6) | data formatting | bytes 1179648

commit v2 on v1

--- a/solution.py
+++ b/solution.py
@@ -12,15 +12,22 @@
 RADIUS = 32
 ROWS = 16
 EARLY = 7
+UNROLL = True
 MESH = pl.DeviceIdType.MESH
 
 
-def spread_ones(slots, orbs):
-    col = np.arange(slots * orbs * orbs)
-    row = np.arange(slots * orbs)[:, None]
-    first = row == col // orbs
-    second = row == (col // (orbs * orbs)) * orbs + col % orbs
-    return jnp.asarray(np.concatenate([first, second], axis=1), jnp.bfloat16)
+def fill_ones(orbs, ones):
+    height, count = ones.shape[0], ones.shape[1] // 2
+    row = lax.broadcasted_iota(jnp.int32, (height, count), 0)
+    col = lax.broadcasted_iota(jnp.int32, (height, count), 1)
+    ahead = col - orbs * row
+    ones[:, :count] = jnp.where((ahead >= 0) & (ahead < orbs), 1.0, 0.0).astype(jnp.bfloat16)
+    line = lax.broadcasted_iota(jnp.int32, (height, 1), 0)
+    slot = lax.div(line, orbs)
+    ahead = col - (orbs * orbs * slot + line - orbs * slot)
+    turns = jnp.floor((ahead.astype(jnp.float32) + 0.5) * (1.0 / orbs)) * orbs
+    hit = (ahead >= 0) & (ahead < orbs * orbs) & (turns == ahead.astype(jnp.float32))
+    ones[:, count:] = jnp.where(hit, 1.0, 0.0).astype(jnp.bfloat16)
 
 
 def fill_maps(coupling, ones, maps_wide, maps):
@@ -108,7 +115,7 @@
 
 
 def kernel(
-    sizes, green_any, near_any, phonon_any, offsets_any, coupling_any, ones_any, out,
+    sizes, green_any, near_any, phonon_any, offsets_any, coupling_any, out,
     green, near, phonon, offsets, coupling, ones, maps_wide, maps, near_all, taken, coupled, wide, recv, res,
     load_sem, near_send, near_recv, in_send, in_recv, out_send, out_recv,
 ):
@@ -125,12 +132,12 @@
         pltpu.make_async_copy(src, dst, load_sem.at[i])
         for i, (src, dst) in enumerate(
             [
-                (coupling_any, coupling), (ones_any, ones), (near_any, near), (green_any, green),
+                (coupling_any, coupling), (near_any, near), (green_any, green),
                 (phonon_any, phonon), (offsets_any, offsets),
             ]
         )
     ]
-    for load in loads[:2]:
+    for load in loads[:3]:
         load.start()
 
     def greet(i, _):
@@ -140,10 +147,20 @@
         )
         return 0
 
-    SCOPE("greet", lambda: lax.fori_loop(1, ne * nk, greet, 0))
-    for load in loads[2:]:
+    def greet_all():
+        for step_e in range(ne):
+            other_e = lax.rem(my_e + step_e, ne)
+            for step_k in range(nk):
+                if step_e or step_k:
+                    pl.semaphore_signal(
+                        barrier, inc=1, device_id=(other_e, lax.rem(my_k + step_k, nk)), device_id_type=MESH
+                    )
+
+    SCOPE("greet", greet_all)
+    for load in loads[3:]:
         load.start()
-    SCOPE("lones", lambda: [loads[0].wait(), loads[1].wait()])
+    SCOPE("lones", lambda: fill_ones(coupling.shape[0], ones))
+    SCOPE("lcoup", lambda: loads[0].wait())
     SCOPE("maps", lambda: fill_maps(coupling, ones, maps_wide, maps))
     flat = nk * block_rows
 
@@ -161,32 +178,46 @@
 
         lax.fori_loop(1, nk, step, 0)
 
-    def in_copies(tile, grp, start):
-        turn, step = tile // ne, tile % ne
-        count = min(ne, tiles - turn * ne)
-        if count == ne:
-            target, target_k = jnp.int32(step), lax.rem(grp + step * nk // ne + turn, nk)
-        else:
-            target, target_k = lax.rem(step + count * grp, ne), grp
-        src = coupled.at[:, pl.ds(tile * ROWS, ROWS), pl.ds(pl.multiple_of(grp * group, 128), group)]
-        dst = recv.at[turn, my_e, my_k]
-        own = (target == my_e) & (target_k == my_k)
-
-        @pl.when(jnp.logical_not(own))
+    full = tiles // ne
+
+    def send_tiles(grp, first, last):
+        lanes = pl.ds(pl.multiple_of(grp * group, 128), group)
+
+        def parts(tile):
+            turn, step = tile // ne, tile % ne
+            count = min(ne, tiles - turn * ne)
+            if count == ne:
+                target, target_k = jnp.int32(step), lax.rem(grp + step * nk // ne + turn, nk)
+            else:
+                target, target_k = lax.rem(step + count * grp, ne), grp
+            src = coupled.at[:, pl.ds(tile * ROWS, ROWS), lanes]
+            dst = recv.at[turn, my_e, my_k]
+
+            def remote():
+                pltpu.make_async_remote_copy(
+                    src_ref=src, dst_ref=dst, send_sem=in_send, recv_sem=in_recv.at[turn],
+                    device_id=(target, target_k), device_id_type=MESH,
+                ).start()
+
+            def local():
+                pltpu.make_async_copy(src, dst, in_recv.at[turn]).start()
+
+            return (target == my_e) & (target_k == my_k), remote, local
+
+        every = [parts(tile) for tile in range(first, last)]
+        ahead = lax.rem(my_k - grp - my_e * nk // ne + 2 * nk, nk)
+        mixed = (ahead < full) | (grp == my_k)
+
+        @pl.when(jnp.logical_not(mixed))
         def _():
-            copy = pltpu.make_async_remote_copy(
-                src_ref=src, dst_ref=dst, send_sem=in_send, recv_sem=in_recv.at[turn],
-                device_id=(target, target_k), device_id_type=MESH,
-            )
-            if start:
-                copy.start()
-            else:
-                copy.wait_send()
-
-        if start:
-            @pl.when(own)
-            def _():
-                pltpu.make_async_copy(src, dst, in_recv.at[turn]).start()
+            for _, remote, _ in every:
+                remote()
+
+        @pl.when(mixed)
+        def _():
+            for own, remote, local in every:
+                pl.when(jnp.logical_not(own))(remote)
+                pl.when(own)(local)
 
     def couple(grp, index):
         base = pl.multiple_of(jnp.clip((grp - 1) * group, 0, atoms - window), 128)
@@ -215,12 +246,10 @@
     early = tiles if rounds == 1 else EARLY
 
     def send_early(grp):
-        for tile in range(early):
-            in_copies(tile, grp, True)
-
-    SCOPE("lgreen", lambda: [load.wait() for load in loads[2:]])
+        send_tiles(grp, 0, early)
+
+    SCOPE("lgreen", lambda: [load.wait() for load in loads[1:]])
     SCOPE("couple0", lambda: couple(my_k, near[...]))
-    SCOPE("small", lambda: fill_wide(small_kernel(phonon, offsets, block_rows), wide))
     SCOPE("barwait", lambda: pl.semaphore_wait(barrier, ne * nk - 1))
     all_others(lambda i: near_copy(i).start())
     send_early(my_k)
@@ -239,11 +268,12 @@
 
     def send_late(i, _):
         grp = paired(my_k, i, nk)
-        for tile in range(early, tiles):
-            in_copies(tile, grp, True)
+        send_tiles(grp, early, tiles)
         return 0
 
     SCOPE("late", lambda: lax.fori_loop(0, nk, send_late, 0))
+
+    SCOPE("small", lambda: fill_wide(small_kernel(phonon, offsets, block_rows), wide))
 
     def mine(turn):
         count = min(ne, tiles - turn * ne)
@@ -251,41 +281,35 @@
             return my_e, lax.rem(my_k + 2 * nk - lax.div(my_e * nk, ne) - turn, nk)
         return lax.rem(my_e + count * (ne - 1) * my_k, ne), my_k
 
-    def out_copies(turn, start, places=tuple(range(ne))):
+    def send_out(turn, place, dst):
+        def remote(target):
+            pltpu.make_async_remote_copy(
+                src_ref=res.at[turn, place, target], dst_ref=dst, send_sem=out_send, recv_sem=out_recv,
+                device_id=(jnp.int32(place), target), device_id_type=MESH,
+            ).start()
+
+        def step(i, _):
+            remote(paired(my_k, jnp.where((my_k // 2 + 1 == nk // 4) | (my_k // 2 == nk // 4), i, nk - i), nk))
+            return 0
+
+        @pl.when(my_e != place)
+        def _():
+            remote(my_k)
+
+        @pl.when(my_e == place)
+        def _():
+            pltpu.make_async_copy(res.at[turn, place, my_k], dst, out_recv).start()
+
+        lax.fori_loop(1, nk, step, 0, unroll=UNROLL)
+
+    def finish(turn):
+        SCOPE("turnwait%d" % turn, lambda: pltpu.make_async_copy(recv.at[turn], recv.at[turn], in_recv.at[turn]).wait())
+        span = flat * ROWS
         step_of, grp_of = mine(turn)
         tile = step_of + turn * ne
         dst = out.at[
             :, pl.ds(pl.multiple_of(tile * ROWS, ROWS), ROWS), pl.ds(pl.multiple_of(grp_of * group, 128), group)
         ]
-
-        def step(i, _):
-            target = paired(my_k, i, nk)
-            for other in places:
-                src = res.at[turn, other, target]
-                own = (other == my_e) & (target == my_k)
-
-                @pl.when(jnp.logical_not(own))
-                def _(src=src, other=other):
-                    copy = pltpu.make_async_remote_copy(
-                        src_ref=src, dst_ref=dst, send_sem=out_send, recv_sem=out_recv,
-                        device_id=(jnp.int32(other), target), device_id_type=MESH,
-                    )
-                    if start:
-                        copy.start()
-                    else:
-                        copy.wait_send()
-
-                if start:
-                    @pl.when(own)
-                    def _(src=src):
-                        pltpu.make_async_copy(src, dst, out_recv).start()
-            return 0
-
-        lax.fori_loop(0, nk, step, 0)
-
-    def finish(turn):
-        SCOPE("turnwait%d" % turn, lambda: pltpu.make_async_copy(recv.at[turn], recv.at[turn], in_recv.at[turn]).wait())
-        span = flat * ROWS
         for place in range(ne):
             low, high = max(place - 1, 0), min(place + 1, ne - 1)
             piece = recv[turn, low : high + 1].reshape((high - low + 1) * span, group)
@@ -295,7 +319,7 @@
                 preferred_element_type=jnp.float32,
             )
             res[turn, place] = value.astype(jnp.bfloat16).reshape(nk, block_rows, ROWS, group)
-            out_copies(turn, True, (place,))
+            send_out(turn, place, dst)
 
     def each_turn(act):
         for turn in range(rounds):
@@ -347,13 +371,12 @@
     flat = nk * block_rows
     vmem = pl.BlockSpec(memory_space=pltpu.VMEM)
     anyw = pl.BlockSpec(memory_space=pl.ANY)
-    ones = spread_ones(slots, coupling.shape[1])
     maps_in = coupling.transpose(1, 0, 2)
     block = (block_rows, ROWS, group)
     result = pl.pallas_call(
         functools.partial(kernel, (ne, nk, window)),
         out_shape=pltpu.VMEM((block_rows, pairs, atoms), jnp.bfloat16),
-        in_specs=[anyw] * 6,
+        in_specs=[anyw] * 5,
         out_specs=vmem,
         scratch_shapes=[
             pltpu.VMEM((block_rows, pairs, atoms), jnp.bfloat16),
@@ -361,7 +384,7 @@
             pltpu.VMEM(phonon.shape, jnp.float32),
             pltpu.SMEM(offsets.shape, jnp.int32),
             pltpu.VMEM(maps_in.shape, jnp.float32),
-            pltpu.VMEM(ones.shape, jnp.bfloat16),
+            pltpu.VMEM((slots * coupling.shape[1], 2 * slots * pairs), jnp.bfloat16),
             pltpu.VMEM((pairs, slots * pairs), jnp.float32),
             pltpu.VMEM((pairs, slots * pairs), jnp.bfloat16),
             pltpu.VMEM((nk, slots, group), jnp.int32),
@@ -370,7 +393,7 @@
             pltpu.VMEM((flat * ROWS, 3 * flat * ROWS), jnp.bfloat16),
             pltpu.VMEM((rounds, ne, nk) + block, jnp.bfloat16),
             pltpu.VMEM((rounds, ne, nk) + block, jnp.bfloat16),
-            pltpu.SemaphoreType.DMA((6,)),
+            pltpu.SemaphoreType.DMA((5,)),
             pltpu.SemaphoreType.DMA,
             pltpu.SemaphoreType.DMA((nk,)),
             pltpu.SemaphoreType.DMA,
@@ -385,7 +408,6 @@
         phonon,
         offsets,
         maps_in,
-        ones,
     )
     return result.reshape(green_blocks.shape)
 

time: 34.9 us -> 34.5 us (0.989)
  Pallas kernels: 33.9 us -> 33.2 us
    pallas_call x1, Pallas kernels: 33.9 us -> 33.2 us  [body(): pl.pallas_call(functools.partial(kernel, (ne, nk, window)), out_shape=plt...]
where the time goes in v2:
time: 34.5 us; the launch traced here: 34 us
  Pallas kernels  33.2 us (96%)
  local copies, waits for them, and re-layouts  0.82 us (2%)
    pallas_call x1, Pallas kernels, body(): pl.pallas_call(functools.partial(kernel, (ne, nk, window)), out_shape=plt...  33.2 us
    unnamed x1, local copies, waits for them, and re-layouts  0.82 us

profile of v2, /device:TPU:0, one launch (start us, length us, event | category | flops | bytes accessed | tf_op | source)
XLA Modules:
  0.0 34.0 jit_solution(2825336701231839583)
XLA Ops:
  0.0 33.2 %shard_map.55 = bf16[2,144,1024]{2,1,0:T(8,128)(2,1)S(1)} custom-call(bf16[2,144,1024]{2,1,0:T(8,128)(2,1)} %bitcast.7, s32[8,128]{1,0:T(8,128)} %bitcast.9, f32[2,8,8]{2,1,0:T(8,128)} %phonon_any.1, s32[8]{0:T(128)} %offsets_any.1, f32[12,8,12]{2,1,0:T(8,128)} %bitcast.8), custom_call_target="tpu_custom_call" | custom-call | tf_op jit(solution)/shard_map/pallas_call | solution.py:376
  33.2 0.8 %copy.8 = bf16[2,1,144,1024]{3,2,1,0:T(8,128)(2,1)} copy(bf16[2,1,144,1024]{3,2,1,0:T(8,128)(2,1)S(1)} %bitcast.6) | data formatting | bytes 1179648

commit v3 on v2

--- a/solution.py
+++ b/solution.py
@@ -267,7 +267,7 @@
     SCOPE("couples", lambda: lax.fori_loop(1, nk, couple_other, 0))
 
     def send_late(i, _):
-        grp = paired(my_k, i, nk)
+        grp = paired(my_k, nk - 1 - i, nk)
         send_tiles(grp, early, tiles)
         return 0
 

time: 34.5 us -> 36.2 us (1.049)
  Pallas kernels: 33.2 us -> 35.2 us
    pallas_call x1, Pallas kernels: 33.2 us -> 35.2 us  [body(): pl.pallas_call(functools.partial(kernel, (ne, nk, window)), out_shape=plt...]
where the time goes in v3:
time: 36.2 us; the launch traced here: 36 us
  Pallas kernels  35.2 us (97%)
  local copies, waits for them, and re-layouts  0.82 us (2%)
    pallas_call x1, Pallas kernels, body(): pl.pallas_call(functools.partial(kernel, (ne, nk, window)), out_shape=plt...  35.2 us
    unnamed x1, local copies, waits for them, and re-layouts  0.82 us

profile of v3, /device:TPU:0, one launch (start us, length us, event | category | flops | bytes accessed | tf_op | source)
XLA Modules:
  0.0 36.0 jit_solution(2404899470655653031)
XLA Ops:
  0.0 35.2 %shard_map.55 = bf16[2,144,1024]{2,1,0:T(8,128)(2,1)S(1)} custom-call(bf16[2,144,1024]{2,1,0:T(8,128)(2,1)} %bitcast.7, s32[8,128]{1,0:T(8,128)} %bitcast.9, f32[2,8,8]{2,1,0:T(8,128)} %phonon_any.1, s32[8]{0:T(128)} %offsets_any.1, f32[12,8,12]{2,1,0:T(8,128)} %bitcast.8), custom_call_target="tpu_custom_call" | custom-call | tf_op jit(solution)/shard_map/pallas_call | solution.py:376
  35.2 0.8 %copy.8 = bf16[2,1,144,1024]{3,2,1,0:T(8,128)(2,1)} copy(bf16[2,1,144,1024]{3,2,1,0:T(8,128)(2,1)S(1)} %bitcast.6) | data formatting | bytes 1179648
